TPU v7x, 256 devices: a whole 4x4x8 slice. The times are simulated.
256 devices in a mesh: dp: 2 (over core), pipe: 8 (over y, x_lo), tensor: 16 (over x_hi, z).
Axes of the slice: x: 4 (x_hi: 2, x_lo: 2; x = x_hi * 2 + x_lo), y: 4, z: 8, core: 2. Of those that a mesh axis runs over, the one named last changes fastest.
Arguments:
- forward_acts: bfloat16 [1024, 8192], P(('dp', 'tensor'), 'pipe'), parts along dimension 0, may hold values from -6 to 6
- backward_grad: bfloat16 [1024, 8192], P(('dp', 'tensor'), 'pipe'), parts along dimension 0, may hold values from -6 to 6
- stored_gate: bfloat16 [1024, 14336], P(('dp', 'pipe'), 'tensor'), parts along dimension 0, may hold values from -8 to 8
- stored_up: bfloat16 [1024, 14336], P(('dp', 'pipe'), 'tensor'), parts along dimension 0, may hold values from -6 to 6
- gate_weight: bfloat16 [8192, 14336], P('pipe', 'tensor'), may hold values from -0.0625 to 0.0625
- up_weight: bfloat16 [8192, 14336], P('pipe', 'tensor'), may hold values from -0.0625 to 0.0625
- down_weight: bfloat16 [14336, 8192], P('tensor', 'pipe'), may hold values from -0.046875 to 0.046875
Outputs:
- layer_output: bfloat16 [1024, 8192], P(('dp', 'tensor'), 'pipe'), parts along dimension 0
- input_grad: bfloat16 [1024, 8192], P(('dp', 'tensor'), 'pipe'), parts along dimension 0
There are 2 independent parts, one for each index of `dp`. A program takes and returns all parts, laid end to end along the dimension named above; an argument that names none is the same for every part. Nothing has to cross between parts.
All inputs are finite; a program needn't handle non-finite values.
Results may differ from a plain program's by a relative error of at most 0.005.
Values may be sent and summed in bfloat16 or wider, within the bound.
A program may use at most 64 MiB of HBM per device.

v0:
```python
import jax
import jax.numpy as jnp
from jax import lax
from jax.sharding import PartitionSpec as P


def make_slopes(hidden_grad, gate_vals, up_vals):
    gate_wide = gate_vals.astype(jnp.float32)
    up_wide = up_vals.astype(jnp.float32)
    sigma = jax.nn.sigmoid(gate_wide)
    gate_slope = (hidden_grad * up_wide * sigma * (1.0 + gate_wide * (1.0 - sigma))).astype(
        jnp.bfloat16
    )
    up_slope = (hidden_grad * gate_wide * sigma).astype(jnp.bfloat16)
    return jnp.concatenate([gate_slope, up_slope], axis=1)


def per_device(
    forward_acts, backward_grad, stored_gate, stored_up, gate_weight, up_weight, down_weight
):
    hidden_width = gate_weight.shape[1]
    contract_last = (((1,), (1,)), ((), ()))
    paired = jnp.concatenate([gate_weight, up_weight], axis=1)
    whole_acts = lax.all_gather(forward_acts, "tensor", axis=0, tiled=True)
    picked = whole_acts
    summed = lax.psum_scatter(
        jnp.dot(picked, paired, preferred_element_type=jnp.float32),
        "pipe",
        scatter_dimension=0,
        tiled=True,
    )
    hidden_part = (jax.nn.silu(summed[:, :hidden_width]) * summed[:, hidden_width:]).astype(
        jnp.bfloat16
    )
    hidden = lax.all_gather(hidden_part, "pipe", axis=0, tiled=True)
    picked = hidden
    layer_output = lax.psum_scatter(
        jnp.dot(picked, down_weight, preferred_element_type=jnp.float32),
        "tensor",
        scatter_dimension=0,
        tiled=True,
    ).astype(jnp.bfloat16)
    whole_grad = lax.all_gather(backward_grad, "tensor", axis=0, tiled=True)
    picked = whole_grad
    hidden_grad = lax.psum_scatter(
        lax.dot_general(picked, down_weight, contract_last, preferred_element_type=jnp.float32),
        "pipe",
        scatter_dimension=0,
        tiled=True,
    )
    local_slopes = make_slopes(hidden_grad, stored_gate, stored_up)
    all_slopes = lax.all_gather(local_slopes, "pipe", axis=0, tiled=True)
    picked = all_slopes
    input_grad = lax.psum_scatter(
        lax.dot_general(picked, paired, contract_last, preferred_element_type=jnp.float32),
        "tensor",
        scatter_dimension=0,
        tiled=True,
    ).astype(jnp.bfloat16)
    return (layer_output, input_grad)


def solution(mesh):
    in_specs = (
        P(("dp", "tensor"), "pipe"),
        P(("dp", "tensor"), "pipe"),
        P(("dp", "pipe"), "tensor"),
        P(("dp", "pipe"), "tensor"),
        P("pipe", "tensor"),
        P("pipe", "tensor"),
        P("tensor", "pipe"),
    )
    out_specs = (P(("dp", "tensor"), "pipe"), P(("dp", "tensor"), "pipe"))
    return jax.shard_map(
        per_device, mesh=mesh, in_specs=in_specs, out_specs=out_specs, check_vma=False
    )
```

profile of v0, /device:TPU:8, one launch (start us, length us, event | category | flops | bytes accessed | tf_op | source)
XLA Modules:
  0.0 779.6 jit_solution(1164099196765025358)
XLA Ops:
  7.2 0.0 copy-start
  7.2 0.0 all-gather.6.cloned.1.call-start
  7.2 0.7 all-gather.6.cloned.1.call-update
  7.9 0.0 copy-start.2
  7.9 0.0 copy-start.3
  7.9 0.0 reduce-scatter.15.cloned.1.call-start
  8.0 84.3 %all-gather.6.cloned.1.call-done = bf16[512,1024]{1,0:T(8,128)(2,1)} async-done(((bf16[32,1024]{1,0:T(8,128)(2,1)}), bf16[512,1024]{1,0:T(8,128)(2,1)}) %all-gather.6.cloned.1.call-update) | async-done | bytes 1048592 | tf_op jit(solution)/shard_map/all_gather | solution.py:43
  92.3 0.0 copy-done
  92.3 3.8 fusion.10
  96.1 0.0 reduce-scatter.15.cloned.1.call-update
  96.1 0.0 all-gather.4.cloned.1.call-start
  96.2 0.7 all-gather.4.cloned.1.call-update
  96.9 0.0 all-gather.8.cloned.1.call-start
  96.9 44.3 %reduce-scatter.15.cloned.1.call-done = f32[64,896]{1,0:T(8,128)} async-done(((f32[512,896]{1,0:T(8,128)}), f32[64,896]{1,0:T(8,128)}) %reduce-scatter.15.cloned.1.call-update) | async-done | bytes 229392 | tf_op jit(solution)/shard_map/reduce_scatter | solution.py:45
  141.2 0.0 copy-done.2
  141.2 0.0 copy-done.3
  141.2 1.1 fusion.5
  142.3 0.7 pad_maximum_fusion
  143.0 0.0 all-gather.8.cloned.1.call-update
  143.0 0.0 reduce-scatter.13.cloned.1.call-start
  143.1 0.0 copy-start.1
  143.1 3.1 constant_dynamic-update-slice_fusion.1
  146.1 0.0 copy-done.1
  146.2 1.4 constant_dynamic-update-slice_fusion
  147.6 76.1 %all-gather.4.cloned.1.call-done = bf16[512,1024]{1,0:T(8,128)(2,1)} async-done(((bf16[32,1024]{1,0:T(8,128)(2,1)}), bf16[512,1024]{1,0:T(8,128)(2,1)}) %all-gather.4.cloned.1.call-update) | async-done | bytes 1048592 | tf_op jit(solution)/shard_map/all_gather | solution.py:24
  223.7 6.3 convolution_bitcast_fusion
  230.0 5.1 copy.23
  235.1 0.0 reduce-scatter.13.cloned.1.call-update
  235.1 0.0 reduce-scatter.11.cloned.1.call-start
  235.2 34.7 %all-gather.8.cloned.1.call-done = bf16[512,1792]{1,0:T(8,128)(2,1)} async-done(((bf16[64,1792]{1,0:T(8,128)(2,1)}), bf16[512,1792]{1,0:T(8,128)(2,1)}) %all-gather.8.cloned.1.call-update) | async-done | bytes 1835024 | tf_op jit(solution)/shard_map/all_gather | solution.py:52
  269.9 6.0 fusion.11
  276.0 0.0 reduce-scatter.11.cloned.1.call-update
  276.0 0.0 reduce-scatter.9.cloned.1.call-start
  276.0 80.3 %reduce-scatter.13.cloned.1.call-done = f32[64,1792]{1,0:T(8,128)} async-done(((f32[512,1792]{1,0:T(8,128)}), f32[64,1792]{1,0:T(8,128)}) %reduce-scatter.13.cloned.1.call-update) | async-done | bytes 458768 | tf_op jit(solution)/shard_map/reduce_scatter | solution.py:26
  356.3 1.1 fusion.8
  357.4 30.6 %all_gather.13 = bf16[512,896]{1,0:T(8,128)(2,1)S(1)} all-gather(bf16[64,896]{1,0:T(8,128)(2,1)S(1)} %fusion.8), channel_id=1, replica_groups=mesh['dp'=2,'pipe'=8,'tensor'=16] {'pipe'}, dimensions={0}, use_global_device_ids=true | all-gather | bytes 1032192 | tf_op jit(solution)/shard_map/all_gather | solution.py:35
  388.1 2.6 fusion.9
  390.7 0.0 reduce-scatter.9.cloned.1.call-update
  390.7 174.5 %reduce-scatter.11.cloned.1.call-done = f32[32,1024]{1,0:T(8,128)} async-done(((f32[512,1024]{1,0:T(8,128)}), f32[32,1024]{1,0:T(8,128)}) %reduce-scatter.11.cloned.1.call-update) | async-done | bytes 131088 | tf_op jit(solution)/shard_map/reduce_scatter | solution.py:54
  565.2 1.5 convert_element_type.27
  566.7 204.5 %reduce-scatter.9.cloned.1.call-done = f32[32,1024]{1,0:T(8,128)} async-done(((f32[512,1024]{1,0:T(8,128)}), f32[32,1024]{1,0:T(8,128)}) %reduce-scatter.9.cloned.1.call-update) | async-done | bytes 131088 | tf_op jit(solution)/shard_map/reduce_scatter | solution.py:37
  771.2 1.5 convert_element_type.22
Async XLA Ops:
  7.2 85.2 %copy-start = (bf16[896,1024]{1,0:T(8,128)(2,1)S(1)}, bf16[896,1024]{1,0:T(8,128)(2,1)}, u32[]{:S(2)}) copy-start(bf16[896,1024]{1,0:T(8,128)(2,1)} %param.13) | copy-start | bytes 5505028
  7.2 85.1 %all-gather.6.cloned.1.call-start = ((), (), s32[]{:S(2)}) async-start(), calls=%async_computation.6 | async-start | bytes 1114112 | tf_op jit(solution)/shard_map/all_gather | solution.py:43
  7.9 133.3 %copy-start.2 = (bf16[64,896]{1,0:T(8,128)(2,1)S(1)}, bf16[64,896]{1,0:T(8,128)(2,1)}, u32[]{:S(2)}) copy-start(bf16[64,896]{1,0:T(8,128)(2,1)} %param.9) | copy-start | bytes 344068
  7.9 133.3 %copy-start.3 = (bf16[64,896]{1,0:T(8,128)(2,1)S(1)}, bf16[64,896]{1,0:T(8,128)(2,1)}, u32[]{:S(2)}) copy-start(bf16[64,896]{1,0:T(8,128)(2,1)} %param.10) | copy-start | bytes 344068
  7.9 133.3 %reduce-scatter.15.cloned.1.call-start = ((), (), s32[]{:S(2)}) async-start(), calls=%async_computation.10 | async-start | bytes 2064384 | tf_op jit(solution)/shard_map/reduce_scatter | solution.py:45
  96.1 127.5 %all-gather.4.cloned.1.call-start = ((), (), s32[]{:S(2)}) async-start(), calls=%async_computation.4 | async-start | bytes 1114112 | tf_op jit(solution)/shard_map/all_gather | solution.py:24
  96.9 173.1 %all-gather.8.cloned.1.call-start = ((), (), s32[]{:S(2)}) async-start(), calls=%async_computation.7 | async-start | bytes 2064384 | tf_op jit(solution)/shard_map/all_gather | solution.py:52
  143.0 213.3 %reduce-scatter.13.cloned.1.call-start = ((), (), s32[]{:S(2)}) async-start(), calls=%async_computation.9 | async-start | bytes 4128768 | tf_op jit(solution)/shard_map/reduce_scatter | solution.py:26
  143.1 3.1 copy-start.1
  235.1 330.0 %reduce-scatter.11.cloned.1.call-start = ((), (), s32[]{:S(2)}) async-start(), calls=%async_computation.8 | async-start | bytes 2228224 | tf_op jit(solution)/shard_map/reduce_scatter | solution.py:54
  276.0 495.2 %reduce-scatter.9.cloned.1.call-start = ((), (), s32[]{:S(2)}) async-start(), calls=%async_computation.5 | async-start | bytes 2228224 | tf_op jit(solution)/shard_map/reduce_scatter | solution.py:37
Sparse Core Ops, SparseCore 0:
  10.6 81.6 all-gather.5
  96.3 44.9 reduce-scatter.14
  143.8 79.8 all-gather.3
  225.3 44.5 all-gather.7
  272.3 83.9 reduce-scatter.12
  360.0 205.0 reduce-scatter.10
  569.1 202.0 reduce-scatter.8
where the time goes:
time: 780 us
  waiting for transfers between devices  700 us (90%)
  blocking collectives  30.6 us (4%)
  matrix products  18.7 us (2%)
  between operations  14.2 us (2%)
  local copies, waits for them, and re-layouts  9.66 us (1%)
    reduce_scatter x1, waiting for transfers between devices, per_device(): lax.psum_scatter(jnp.dot(picked, down_weight, preferred_element_type=jnp....  204 us
    reduce_scatter x1, waiting for transfers between devices, per_device(): lax.psum_scatter(lax.dot_general(picked, paired, contract_last, preferred...  174 us
    all_gather x1, waiting for transfers between devices, per_device(): whole_grad = lax.all_gather(backward_grad, 'tensor', axis=0, tiled=True)  84.3 us
    reduce_scatter x1, waiting for transfers between devices, per_device(): lax.psum_scatter(jnp.dot(picked, paired, preferred_element_type=jnp.float...  80.3 us
    all_gather x1, waiting for transfers between devices, per_device(): whole_acts = lax.all_gather(forward_acts, 'tensor', axis=0, tiled=True)  76.1 us
    reduce_scatter x1, waiting for transfers between devices, per_device(): lax.psum_scatter(lax.dot_general(picked, down_weight, contract_last, pref...  44.3 us
    all_gather x1, waiting for transfers between devices, per_device(): all_slopes = lax.all_gather(local_slopes, 'pipe', axis=0, tiled=True)  34.7 us
    all_gather x1, blocking collectives, per_device(): hidden = lax.all_gather(hidden_part, 'pipe', axis=0, tiled=True)  30.6 us
  transfers between devices with their start and end apart: 7, of which 7 were waited for; matrix products, arithmetic and copies ran while one was open for 4% of the time, Pallas kernels for 0%

commit v1 on v0

--- a/solution.py
+++ b/solution.py
@@ -40,7 +40,8 @@
         scatter_dimension=0,
         tiled=True,
     ).astype(jnp.bfloat16)
-    whole_grad = lax.all_gather(backward_grad, "tensor", axis=0, tiled=True)
+    y = lax.all_to_all(jnp.stack([backward_grad] * lax.psum(1, "tensor")), "tensor", 0, 0)
+    whole_grad = jnp.concatenate(y, axis=0)
     picked = whole_grad
     hidden_grad = lax.psum_scatter(
         lax.dot_general(picked, down_weight, contract_last, preferred_element_type=jnp.float32),

time: 780 us -> 671 us (0.86)
  waiting for transfers between devices: 700 us -> 550 us
  blocking collectives: 30.6 us -> 70.4 us
    all_gather x1 -> x0, waiting for transfers between devices: 84.3 us -> none  [per_device(): whole_grad = lax.all_gather(backward_grad, 'tensor', axis=0, tiled=True)]
    reduce_scatter x1, waiting for transfers between devices: 80.3 us -> 13.7 us  [per_device(): lax.psum_scatter(jnp.dot(picked, paired, preferred_element_type=jnp.float...]
    all_gather x1, waiting for transfers between devices: 34.7 us -> 84.1 us  [per_device(): all_slopes = lax.all_gather(local_slopes, 'pipe', axis=0, tiled=True)]
    all_gather x1, waiting for transfers between devices: 76.1 us -> 28.4 us  [per_device(): whole_acts = lax.all_gather(forward_acts, 'tensor', axis=0, tiled=True)]
    all_to_all x0 -> x1, blocking collectives: none -> 39.3 us  [per_device(): lax.all_to_all(jnp.stack([backward_grad] * lax.psum(1, 'tensor')), 'tenso...]
  transfers between devices with their start and end apart: 7 -> 6, of which waited for: 7 -> 6; matrix products, arithmetic and copies ran while one was open for 4% -> 4% of each run, Pallas kernels for 0% -> 0%
where the time goes in v1:
time: 671 us
  waiting for transfers between devices  550 us (82%)
  blocking collectives  70.4 us (10%)
  matrix products  17.5 us (3%)
  between operations  15.3 us (2%)
  local copies, waits for them, and re-layouts  10.9 us (2%)
    reduce_scatter x1, waiting for transfers between devices, per_device(): lax.psum_scatter(jnp.dot(picked, down_weight, preferred_element_type=jnp....  204 us
    reduce_scatter x1, waiting for transfers between devices, per_device(): lax.psum_scatter(lax.dot_general(picked, paired, contract_last, preferred...  174 us
    all_gather x1, waiting for transfers between devices, per_device(): all_slopes = lax.all_gather(local_slopes, 'pipe', axis=0, tiled=True)  84.1 us
    reduce_scatter x1, waiting for transfers between devices, per_device(): lax.psum_scatter(lax.dot_general(picked, down_weight, contract_last, pref...  45 us
    all_to_all x1, blocking collectives, per_device(): lax.all_to_all(jnp.stack([backward_grad] * lax.psum(1, 'tensor')), 'tenso...  39.3 us
    all_gather x1, blocking collectives, per_device(): hidden = lax.all_gather(hidden_part, 'pipe', axis=0, tiled=True)  31.1 us
    all_gather x1, waiting for transfers between devices, per_device(): whole_acts = lax.all_gather(forward_acts, 'tensor', axis=0, tiled=True)  28.4 us
    reduce_scatter x1, waiting for transfers between devices, per_device(): lax.psum_scatter(jnp.dot(picked, paired, preferred_element_type=jnp.float...  13.7 us
  transfers between devices with their start and end apart: 6, of which 6 were waited for; matrix products, arithmetic and copies ran while one was open for 4% of the time, Pallas kernels for 0%

profile of v1, /device:TPU:8, one launch (start us, length us, event | category | flops | bytes accessed | tf_op | source)
XLA Modules:
  0.0 670.6 jit_solution(11660282268850565930)
XLA Ops:
  8.0 0.0 copy-start
  8.0 0.0 reduce-scatter.15.cloned.1.call-start
  8.1 1.1 stack.2
  9.1 39.3 %all_to_all.5 = bf16[16,32,1024]{2,1,0:T(8,128)(2,1)S(1)} all-to-all(bf16[16,32,1024]{2,1,0:T(8,128)(2,1)S(1)} %stack.2), channel_id=1, replica_groups=mesh['dp'=2,'pipe'=8,'tensor'=16] {'tensor'}, dimensions={0} | all-to-all | bytes 2097152 | tf_op jit(solution)/shard_map/all_to_all | solution.py:43
  48.4 0.0 copy-done
  48.4 0.0 copy-start.2
  48.4 0.0 copy-start.3
  48.4 2.5 fusion.10
  51.0 0.0 reduce-scatter.15.cloned.1.call-update
  51.0 0.0 all-gather.3.cloned.1.call-start
  51.0 0.5 all-gather.3.cloned.1.call-update
  51.6 0.0 all-gather.5.cloned.1.call-start
  51.6 45.0 %reduce-scatter.15.cloned.1.call-done = f32[64,896]{1,0:T(8,128)} async-done(((f32[512,896]{1,0:T(8,128)}), f32[64,896]{1,0:T(8,128)}) %reduce-scatter.15.cloned.1.call-update) | async-done | bytes 229392 | tf_op jit(solution)/shard_map/reduce_scatter | solution.py:46
  96.6 0.0 copy-done.2
  96.6 0.0 copy-done.3
  96.6 1.1 fusion.5
  97.7 0.7 pad_maximum_fusion
  98.4 0.0 all-gather.5.cloned.1.call-update
  98.4 0.0 reduce-scatter.13.cloned.1.call-start
  98.5 0.0 copy-start.1
  98.5 3.1 constant_dynamic-update-slice_fusion.1
  101.6 0.0 copy-done.1
  101.6 1.5 constant_dynamic-update-slice_fusion
  103.1 28.4 %all-gather.3.cloned.1.call-done = bf16[512,1024]{1,0:T(8,128)(2,1)} async-done(((bf16[32,1024]{1,0:T(8,128)(2,1)}), bf16[512,1024]{1,0:T(8,128)(2,1)}) %all-gather.3.cloned.1.call-update) | async-done | bytes 1048592 | tf_op jit(solution)/shard_map/all_gather | solution.py:24
  131.6 6.3 convolution_bitcast_fusion
  137.8 5.2 copy.23
  143.0 0.0 reduce-scatter.13.cloned.1.call-update
  143.0 0.0 reduce-scatter.11.cloned.1.call-start
  143.1 84.1 %all-gather.5.cloned.1.call-done = bf16[512,1792]{1,0:T(8,128)(2,1)} async-done(((bf16[64,1792]{1,0:T(8,128)(2,1)}), bf16[512,1792]{1,0:T(8,128)(2,1)}) %all-gather.5.cloned.1.call-update) | async-done | bytes 1835024 | tf_op jit(solution)/shard_map/all_gather | solution.py:53
  227.2 6.0 fusion.11
  233.3 0.0 reduce-scatter.11.cloned.1.call-update
  233.3 0.0 reduce-scatter.9.cloned.1.call-start
  233.4 13.7 %reduce-scatter.13.cloned.1.call-done = f32[64,1792]{1,0:T(8,128)} async-done(((f32[512,1792]{1,0:T(8,128)}), f32[64,1792]{1,0:T(8,128)}) %reduce-scatter.13.cloned.1.call-update) | async-done | bytes 458768 | tf_op jit(solution)/shard_map/reduce_scatter | solution.py:26
  247.1 1.1 fusion.8
  248.2 31.1 %all_gather.10 = bf16[512,896]{1,0:T(8,128)(2,1)S(1)} all-gather(bf16[64,896]{1,0:T(8,128)(2,1)S(1)} %fusion.8), channel_id=1, replica_groups=mesh['dp'=2,'pipe'=8,'tensor'=16] {'pipe'}, dimensions={0}, use_global_device_ids=true | all-gather | bytes 1032192 | tf_op jit(solution)/shard_map/all_gather | solution.py:35
  279.3 2.6 fusion.9
  281.9 0.0 reduce-scatter.9.cloned.1.call-update
  281.9 174.2 %reduce-scatter.11.cloned.1.call-done = f32[32,1024]{1,0:T(8,128)} async-done(((f32[512,1024]{1,0:T(8,128)}), f32[32,1024]{1,0:T(8,128)}) %reduce-scatter.11.cloned.1.call-update) | async-done | bytes 131088 | tf_op jit(solution)/shard_map/reduce_scatter | solution.py:55
  456.1 1.5 convert_element_type.27
  457.7 204.3 %reduce-scatter.9.cloned.1.call-done = f32[32,1024]{1,0:T(8,128)} async-done(((f32[512,1024]{1,0:T(8,128)}), f32[32,1024]{1,0:T(8,128)}) %reduce-scatter.9.cloned.1.call-update) | async-done | bytes 131088 | tf_op jit(solution)/shard_map/reduce_scatter | solution.py:37
  662.0 1.5 convert_element_type.22
Async XLA Ops:
  8.0 40.4 %copy-start = (bf16[896,1024]{1,0:T(8,128)(2,1)S(1)}, bf16[896,1024]{1,0:T(8,128)(2,1)}, u32[]{:S(2)}) copy-start(bf16[896,1024]{1,0:T(8,128)(2,1)} %param.13) | copy-start | bytes 5505028
  8.0 88.6 %reduce-scatter.15.cloned.1.call-start = ((), (), s32[]{:S(2)}) async-start(), calls=%async_computation.10 | async-start | bytes 2064384 | tf_op jit(solution)/shard_map/reduce_scatter | solution.py:46
  48.4 48.2 %copy-start.2 = (bf16[64,896]{1,0:T(8,128)(2,1)S(1)}, bf16[64,896]{1,0:T(8,128)(2,1)}, u32[]{:S(2)}) copy-start(bf16[64,896]{1,0:T(8,128)(2,1)} %param.9) | copy-start | bytes 344068
  48.4 48.2 %copy-start.3 = (bf16[64,896]{1,0:T(8,128)(2,1)S(1)}, bf16[64,896]{1,0:T(8,128)(2,1)}, u32[]{:S(2)}) copy-start(bf16[64,896]{1,0:T(8,128)(2,1)} %param.10) | copy-start | bytes 344068
  51.0 80.6 %all-gather.3.cloned.1.call-start = ((), (), s32[]{:S(2)}) async-start(), calls=%async_computation.5 | async-start | bytes 1114112 | tf_op jit(solution)/shard_map/all_gather | solution.py:24
  51.6 175.7 %all-gather.5.cloned.1.call-start = ((), (), s32[]{:S(2)}) async-start(), calls=%async_computation.7 | async-start | bytes 2064384 | tf_op jit(solution)/shard_map/all_gather | solution.py:53
  98.4 148.7 %reduce-scatter.13.cloned.1.call-start = ((), (), s32[]{:S(2)}) async-start(), calls=%async_computation.9 | async-start | bytes 4128768 | tf_op jit(solution)/shard_map/reduce_scatter | solution.py:26
  98.5 3.1 copy-start.1
  143.0 313.1 %reduce-scatter.11.cloned.1.call-start = ((), (), s32[]{:S(2)}) async-start(), calls=%async_computation.8 | async-start | bytes 2228224 | tf_op jit(solution)/shard_map/reduce_scatter | solution.py:55
  233.3 428.7 %reduce-scatter.9.cloned.1.call-start = ((), (), s32[]{:S(2)}) async-start(), calls=%async_computation.6 | async-start | bytes 2228224 | tf_op jit(solution)/shard_map/reduce_scatter | solution.py:37
Sparse Core Ops, SparseCore 0:
  51.1 45.4 reduce-scatter.14
  143.2 103.8 reduce-scatter.12
  251.0 205.1 reduce-scatter.10
  459.9 202.0 reduce-scatter.8
Sparse Core Ops, SparseCore 1:
  54.0 77.5 all-gather.2
  133.2 94.0 all-gather.4
